TPU v7x, 32 devices: a whole 2x2x4 slice. The times are simulated.
32 devices in a mesh: dp: 8 (over y, x, core), expert: 4 (over z).
Axes of the slice: x: 2, y: 2, z: 4, core: 2. Of those that a mesh axis runs over, the one named last changes fastest.
Arguments:
- tokens: bfloat16 [12288, 1024], P(('dp', 'expert')), may hold values from -6 to 6
- cotangent: bfloat16 [12288, 1024], P(('dp', 'expert')), may hold values from -6 to 6
- routes: int32 [12288, 8], P(('dp', 'expert')), may hold values from 0 to 15, all different within a row; in each aligned block of 384 rows (0 to 383, 384 to 767, ...) at most 256 rows name the same one
- cont_ids: int32 [32, 128], P(('dp', 'expert')), may hold values from 0 to 1, never falling along the last dimension, each value on 1 to 96 neighbouring positions
- norm_gains: float32 [1024, 2], replicated, may hold values from 0.5 to 1.5
- gains_moment: float32 [1024, 2], P(('dp', 'expert')), may hold values from -192 to 192
- gains_average: float32 [1024, 2], P(('dp', 'expert')), may hold values from 0.5 to 1.5
- heads_in: bfloat16 [1024, 2048], replicated, may hold values from -0.5 to 0.5
- heads_in_master: float32 [1024, 2048], P(('dp', 'expert')), may hold values from -0.625 to 0.625
- heads_in_moment: float32 [1024, 2048], P(('dp', 'expert')), may hold values from -128 to 128
- heads_in_average: float32 [1024, 2048], P(('dp', 'expert')), may hold values from -0.625 to 0.625
- heads_out: bfloat16 [1024, 1024], replicated, may hold values from -1.5 to 1.5
- heads_out_master: float32 [1024, 1024], P(('dp', 'expert')), may hold values from -0.1875 to 0.1875
- heads_out_moment: float32 [1024, 1024], P(('dp', 'expert')), may hold values from -32 to 32
- heads_out_average: float32 [1024, 1024], P(('dp', 'expert')), may hold values from -0.1875 to 0.1875
- router: bfloat16 [1024, 16], replicated, may hold values from -0.09375 to 0.09375
- router_master: float32 [1024, 16], P(('dp', 'expert')), may hold values from -2.5 to 2.5
- router_moment: float32 [1024, 16], P(('dp', 'expert')), may hold values from -128 to 128
- router_average: float32 [1024, 16], P(('dp', 'expert')), may hold values from -2.5 to 2.5
- expert_in: bfloat16 [16, 1024, 1024], P('expert'), may hold values from -0.1875 to 0.1875
- expert_in_master: float32 [16, 1024, 1024], P('expert', 'dp'), may hold values from -0.25 to 0.25
- expert_in_moment: float32 [16, 1024, 1024], P('expert', 'dp'), may hold values from -16 to 16
- expert_in_average: float32 [16, 1024, 1024], P('expert', 'dp'), may hold values from -0.25 to 0.25
- expert_out: bfloat16 [16, 1024, 512], P('expert'), may hold values from -1 to 1
- expert_out_master: float32 [16, 1024, 512], P('expert', 'dp'), may hold values from -0.0546875 to 0.0546875
- expert_out_moment: float32 [16, 1024, 512], P('expert', 'dp'), may hold values from -3.5 to 3.5
- expert_out_average: float32 [16, 1024, 512], P('expert', 'dp'), may hold values from -0.0546875 to 0.0546875
Outputs:
- output: bfloat16 [12288, 1024], P(('dp', 'expert'))
- token_grad: float32 [12288, 1024], P(('dp', 'expert'))
- gains_next: float32 [1024, 2], P(('dp', 'expert'))
- gains_moment_next: float32 [1024, 2], P(('dp', 'expert'))
- gains_average_next: float32 [1024, 2], P(('dp', 'expert'))
- heads_in_next: float32 [1024, 2048], P(('dp', 'expert'))
- heads_in_moment_next: float32 [1024, 2048], P(('dp', 'expert'))
- heads_in_average_next: float32 [1024, 2048], P(('dp', 'expert'))
- heads_out_next: float32 [1024, 1024], P(('dp', 'expert'))
- heads_out_moment_next: float32 [1024, 1024], P(('dp', 'expert'))
- heads_out_average_next: float32 [1024, 1024], P(('dp', 'expert'))
- router_next: float32 [1024, 16], P(('dp', 'expert'))
- router_moment_next: float32 [1024, 16], P(('dp', 'expert'))
- router_average_next: float32 [1024, 16], P(('dp', 'expert'))
- expert_in_next: float32 [16, 1024, 1024], P('expert', 'dp')
- expert_in_moment_next: float32 [16, 1024, 1024], P('expert', 'dp')
- expert_in_average_next: float32 [16, 1024, 1024], P('expert', 'dp')
- expert_out_next: float32 [16, 1024, 512], P('expert', 'dp')
- expert_out_moment_next: float32 [16, 1024, 512], P('expert', 'dp')
- expert_out_average_next: float32 [16, 1024, 512], P('expert', 'dp')
Inputs may be any that keep to these rules, and one draw needn't show every extreme that they name: `routes`: each row names 8 different experts. Among the tokens of one group no expert is named more than 256 times, a bound that some block reaches. `cont_ids`: in each row the numbers never fall; each of the 2 continuations has 1 to 96 tokens.
All inputs are finite; a program needn't handle non-finite values.
Results may differ from a plain program's by a relative error of at most 0.017.
Values may be sent and summed in bfloat16 or wider, within the bound.
A program may use at most 256 MiB of HBM per device.

v0:
```python
import jax
import jax.numpy as jnp
from jax import lax
from jax.sharding import PartitionSpec as P

HEADS = 16
KV_HEADS = 8
HEAD_DIM = 64
EPS = 1e-06
SCALE = 0.015625
THETA = 10000.0
MOMENTUM = 0.9
DECAY = 0.8
RATE = 0.001
HIGHEST = lax.Precision.HIGHEST


def layout(labels_row, prompt_len):
    places = jnp.arange(prompt_len + labels_row.shape[0], dtype=jnp.int32)
    earlier = jnp.sum((labels_row[None, :] < labels_row[:, None]).astype(jnp.int32), axis=1)
    offset = places[prompt_len:] - prompt_len - earlier
    positions = jnp.concatenate([places[:prompt_len], prompt_len + offset]).astype(jnp.float32)
    labels = jnp.concatenate([jnp.full((prompt_len,), -1, jnp.int32), labels_row])
    allowed = (places[None, :] <= places[:, None]) & (
        (places[None, :] < prompt_len) | (labels[None, :] == labels[:, None])
    )
    return (positions, allowed)


def rope_tables(positions):
    middle = HEAD_DIM // 2
    frequency = THETA ** (-2.0 * jnp.arange(middle, dtype=jnp.float32) / HEAD_DIM)
    angles = positions[:, None] * frequency[None, :]
    angles = jnp.concatenate([angles, angles], axis=1)
    return (jnp.cos(angles)[:, None, :], jnp.sin(angles)[:, None, :])


def rotate(values, cosine, sine_table):
    middle = values.shape[-1] // 2
    turned = jnp.concatenate([-values[..., middle:], values[..., :middle]], axis=-1)
    return values * cosine + turned * sine_table


def unrotate(gradient, cosine, sine_table):
    middle = gradient.shape[-1] // 2
    shifted = gradient * sine_table
    return gradient * cosine + jnp.concatenate(
        [shifted[..., middle:], -shifted[..., :middle]], axis=-1
    )


def masked_scores(queries, key_rows, allowed):
    products = (
        jnp.einsum("qkgd,pkd->kgqp", queries, key_rows, preferred_element_type=jnp.float32) * SCALE
    )
    return jnp.where(allowed[None, None], products, -1e30)


def rms_parts(values, gain):
    factor = lax.rsqrt(jnp.mean(values * values, axis=-1, keepdims=True) + EPS)
    return (values * factor * gain, factor)


def rms_back(incoming, values, factor, gain):
    normed = values * factor
    gain_grad = jnp.sum(incoming * normed, axis=0)
    weighted = incoming * gain
    input_grad = factor * (weighted - normed * jnp.mean(weighted * normed, axis=-1, keepdims=True))
    return (input_grad, gain_grad)


def bank_total(values, scales, bank_hot):
    partial_value = jnp.einsum(
        "tk,tkp,tkd->tpd", scales, bank_hot, values.astype(jnp.float32), precision=HIGHEST
    )
    return jnp.sum(partial_value.astype(jnp.bfloat16).astype(jnp.float32), axis=1)


def update(gradient, master, moment, average):
    moment_next = MOMENTUM * moment + gradient
    master_next = master - RATE * (gradient + MOMENTUM * moment_next)
    return (master_next, moment_next, DECAY * average + (1.0 - DECAY) * master_next)


def body(
    tokens,
    cotangent,
    routes,
    cont_ids,
    norm_gains,
    gains_moment,
    gains_average,
    heads_in,
    heads_in_master,
    heads_in_moment,
    heads_in_average,
    heads_out,
    heads_out_master,
    heads_out_moment,
    heads_out_average,
    router,
    router_master,
    router_moment,
    router_average,
    expert_in,
    expert_in_master,
    expert_in_moment,
    expert_in_average,
    expert_out,
    expert_out_master,
    expert_out_moment,
    expert_out_average,
):
    token_count, model_width = tokens.shape
    fanout = routes.shape[1]
    local_experts = expert_in.shape[0]
    peer_count = lax.axis_size("expert")
    experts = local_experts * peer_count
    capacity = 4 * token_count * fanout // (3 * experts)
    ff_width = expert_out.shape[2]
    group_size = HEADS // KV_HEADS
    query_end = HEADS * HEAD_DIM
    key_end = query_end + KV_HEADS * HEAD_DIM
    token_rows = tokens.astype(jnp.float32)
    normed_one, factor_one = rms_parts(token_rows, norm_gains[:, 0])
    first_in = normed_one.astype(jnp.bfloat16)
    projected = jnp.dot(first_in, heads_in, preferred_element_type=jnp.float32)
    positions, allowed = layout(cont_ids[0], token_count - cont_ids.shape[1])
    cosine, sine_table = rope_tables(positions)
    queries = rotate(
        projected[:, :query_end].reshape(token_count, HEADS, HEAD_DIM), cosine, sine_table
    )
    queries = queries.astype(jnp.bfloat16).reshape(token_count, KV_HEADS, group_size, HEAD_DIM)
    key_rows = rotate(
        projected[:, query_end:key_end].reshape(token_count, KV_HEADS, HEAD_DIM), cosine, sine_table
    ).astype(jnp.bfloat16)
    value_rows = (
        projected[:, key_end:].reshape(token_count, KV_HEADS, HEAD_DIM).astype(jnp.bfloat16)
    )
    scores = masked_scores(queries, key_rows, allowed)
    row_peak = jnp.max(scores, axis=-1, keepdims=True)
    log_total = row_peak + jnp.log(jnp.sum(jnp.exp(scores - row_peak), axis=-1, keepdims=True))
    weights = jnp.exp(scores - log_total).astype(jnp.bfloat16)
    attended = jnp.einsum("kgqp,pkd->qkgd", weights, value_rows, preferred_element_type=jnp.float32)
    attended = attended.reshape(token_count, query_end).astype(jnp.bfloat16)
    branch = jnp.einsum("th,dh->td", attended, heads_out, preferred_element_type=jnp.float32)
    hidden = token_rows + branch
    normed_two, factor_two = rms_parts(hidden, norm_gains[:, 1])
    second_in = normed_two.astype(jnp.bfloat16)
    logits = jnp.dot(second_in, router, preferred_element_type=jnp.float32)
    gate_probs = jax.nn.softmax(jnp.take_along_axis(logits, routes, axis=1), axis=-1)
    incoming = cotangent.astype(jnp.float32)
    matches = (routes[:, :, None] == jnp.arange(experts, dtype=jnp.int32)[None, None, :]).astype(
        jnp.int32
    )
    counts = jnp.sum(matches, axis=1)
    before = jnp.cumsum(counts, axis=0) - counts
    flat_rows = routes * capacity + jnp.take_along_axis(before, routes, axis=1)
    token_ids = jnp.broadcast_to(jnp.arange(token_count, dtype=jnp.int32)[:, None], routes.shape)
    slot_tokens = (
        jnp.full((experts * capacity,), token_count, jnp.int32)
        .at[flat_rows.reshape(-1)]
        .set(token_ids.reshape(-1))
    )
    slot_picks = (
        jnp.full((experts * capacity,), token_count * fanout, jnp.int32)
        .at[flat_rows.reshape(-1)]
        .set(jnp.arange(token_count * fanout, dtype=jnp.int32))
    )
    slot_gates = jnp.take(gate_probs.reshape(-1), slot_picks, axis=0, mode="fill", fill_value=0.0)
    peer_ids = jnp.arange(peer_count, dtype=jnp.int32)
    owners = routes // local_experts
    bank_hot = (owners[:, :, None] == peer_ids[None, None, :]).astype(jnp.float32)
    outgoing = jnp.take(second_in, slot_tokens, axis=0, mode="fill", fill_value=0).reshape(
        experts, capacity, model_width
    )
    inputs = lax.all_to_all(outgoing, "expert", split_axis=0, concat_axis=1, tiled=True)
    gate_up = jnp.einsum("erd,edf->erf", inputs, expert_in, preferred_element_type=jnp.float32)
    gate_part = gate_up[..., :ff_width]
    up_part = gate_up[..., ff_width:]
    activated = (jax.nn.silu(gate_part) * up_part).astype(jnp.bfloat16)
    result = jnp.einsum(
        "erf,edf->erd", activated, expert_out, preferred_element_type=jnp.float32
    ).astype(jnp.bfloat16)
    returned = lax.all_to_all(result, "expert", split_axis=1, concat_axis=0, tiled=True).reshape(
        experts * capacity, model_width
    )
    chosen = jnp.take(returned, flat_rows.reshape(-1), axis=0).reshape(
        token_count, fanout, model_width
    )
    mixture = bank_total(chosen, gate_probs, bank_hot)
    grad_gates = jnp.einsum("td,tkd->tk", cotangent, chosen, preferred_element_type=jnp.float32)
    outgoing_grads = (
        slot_gates[:, None] * jnp.take(cotangent, slot_tokens, axis=0, mode="fill", fill_value=0)
    ).astype(jnp.bfloat16)
    grad_result = lax.all_to_all(
        outgoing_grads.reshape(experts, capacity, model_width),
        "expert",
        split_axis=0,
        concat_axis=1,
        tiled=True,
    )
    output = (hidden + mixture).astype(jnp.bfloat16)
    grad_activated = jnp.einsum(
        "erd,edf->erf", grad_result, expert_out, preferred_element_type=jnp.float32
    )
    sigmoid_gate = jax.nn.sigmoid(gate_part)
    grad_gate_part = (
        grad_activated * up_part * sigmoid_gate * (1.0 + gate_part * (1.0 - sigmoid_gate))
    )
    grad_up_part = grad_activated * (gate_part * sigmoid_gate)
    grad_gate_up = jnp.concatenate([grad_gate_part, grad_up_part], axis=-1).astype(jnp.bfloat16)
    grad_expert_out = jnp.einsum(
        "erd,erf->edf", grad_result, activated, preferred_element_type=jnp.float32
    )
    grad_expert_in = jnp.einsum(
        "erd,erf->edf", inputs, grad_gate_up, preferred_element_type=jnp.float32
    )
    grad_inputs = jnp.einsum(
        "erf,edf->erd", grad_gate_up, expert_in, preferred_element_type=jnp.float32
    ).astype(jnp.bfloat16)
    returned_grads = lax.all_to_all(
        grad_inputs, "expert", split_axis=1, concat_axis=0, tiled=True
    ).reshape(experts * capacity, model_width)
    gathered_grads = jnp.take(returned_grads, flat_rows.reshape(-1), axis=0).reshape(
        token_count, fanout, model_width
    )
    grad_second = bank_total(gathered_grads, jnp.ones((token_count, fanout), jnp.float32), bank_hot)
    weighted_sum = jnp.sum(gate_probs * grad_gates, axis=1, keepdims=True)
    grad_picked = gate_probs * (grad_gates - weighted_sum)
    grad_logits = jnp.einsum(
        "tk,tke->te", grad_picked, matches.astype(jnp.float32), precision=HIGHEST
    )
    grad_router = jnp.dot(second_in.astype(jnp.float32).T, grad_logits, precision=HIGHEST)
    grad_second = grad_second + jnp.dot(
        grad_logits, router.astype(jnp.float32).T, precision=HIGHEST
    )
    grad_hidden_norm, grad_gain_two = rms_back(grad_second, hidden, factor_two, norm_gains[:, 1])
    grad_hidden = incoming + grad_hidden_norm
    grad_branch = grad_hidden.astype(jnp.bfloat16)
    grad_heads_out = jnp.einsum(
        "td,th->dh", grad_branch, attended, preferred_element_type=jnp.float32
    )
    grad_attended = jnp.dot(grad_branch, heads_out, preferred_element_type=jnp.float32).astype(
        jnp.bfloat16
    )
    grad_attended = grad_attended.reshape(token_count, KV_HEADS, group_size, HEAD_DIM)
    weight_full = jnp.exp(masked_scores(queries, key_rows, allowed) - log_total)
    grad_weights = jnp.einsum(
        "qkgd,pkd->kgqp", grad_attended, value_rows, preferred_element_type=jnp.float32
    )
    spread = jnp.sum(weight_full * grad_weights, axis=-1, keepdims=True)
    grad_scores = (weight_full * (grad_weights - spread)).astype(jnp.bfloat16)
    grad_queries = (
        jnp.einsum("kgqp,pkd->qkgd", grad_scores, key_rows, preferred_element_type=jnp.float32)
        * SCALE
    )
    grad_keys = (
        jnp.einsum("kgqp,qkgd->pkd", grad_scores, queries, preferred_element_type=jnp.float32)
        * SCALE
    )
    grad_values = jnp.einsum(
        "kgqp,qkgd->pkd",
        weight_full.astype(jnp.bfloat16),
        grad_attended,
        preferred_element_type=jnp.float32,
    )
    grad_projected = jnp.concatenate(
        [
            unrotate(
                grad_queries.reshape(token_count, HEADS, HEAD_DIM), cosine, sine_table
            ).reshape(token_count, query_end),
            unrotate(grad_keys, cosine, sine_table).reshape(token_count, KV_HEADS * HEAD_DIM),
            grad_values.reshape(token_count, KV_HEADS * HEAD_DIM),
        ],
        axis=1,
    ).astype(jnp.bfloat16)
    grad_heads_in = jnp.einsum(
        "td,tc->dc", first_in, grad_projected, preferred_element_type=jnp.float32
    )
    grad_first = jnp.einsum(
        "tc,dc->td", grad_projected, heads_in, preferred_element_type=jnp.float32
    )
    grad_tokens_norm, grad_gain_one = rms_back(grad_first, token_rows, factor_one, norm_gains[:, 0])
    token_grad = grad_hidden + grad_tokens_norm
    grad_gains = jnp.stack([grad_gain_one, grad_gain_two], axis=1)
    summed = (
        lax.psum_scatter(grad_heads_in, ("dp", "expert"), scatter_dimension=0, tiled=True),
        lax.psum_scatter(grad_heads_out, ("dp", "expert"), scatter_dimension=0, tiled=True),
        lax.psum_scatter(grad_router, ("dp", "expert"), scatter_dimension=0, tiled=True),
        lax.psum_scatter(grad_gains, ("dp", "expert"), scatter_dimension=0, tiled=True),
    )
    expert_sums = (
        lax.psum_scatter(
            grad_expert_in.astype(jnp.bfloat16), "dp", scatter_dimension=1, tiled=True
        ).astype(jnp.float32),
        lax.psum_scatter(
            grad_expert_out.astype(jnp.bfloat16), "dp", scatter_dimension=1, tiled=True
        ).astype(jnp.float32),
    )
    shard_rows = model_width // lax.axis_size(("dp", "expert"))
    gains_share = lax.dynamic_slice_in_dim(
        norm_gains, lax.axis_index(("dp", "expert")) * shard_rows, shard_rows, 0
    )
    gains_new = update(summed[3], gains_share, gains_moment, gains_average)
    inproj_new = update(summed[0], heads_in_master, heads_in_moment, heads_in_average)
    outproj_new = update(summed[1], heads_out_master, heads_out_moment, heads_out_average)
    router_new = update(summed[2], router_master, router_moment, router_average)
    upper_new = update(expert_sums[0], expert_in_master, expert_in_moment, expert_in_average)
    lower_new = update(expert_sums[1], expert_out_master, expert_out_moment, expert_out_average)
    return (
        output,
        token_grad,
        gains_new[0],
        gains_new[1],
        gains_new[2],
        inproj_new[0],
        inproj_new[1],
        inproj_new[2],
        outproj_new[0],
        outproj_new[1],
        outproj_new[2],
        router_new[0],
        router_new[1],
        router_new[2],
        upper_new[0],
        upper_new[1],
        upper_new[2],
        lower_new[0],
        lower_new[1],
        lower_new[2],
    )


def solution(mesh):
    return jax.shard_map(
        body,
        mesh=mesh,
        in_specs=(
            P(("dp", "expert"), None),
            P(("dp", "expert"), None),
            P(("dp", "expert"), None),
            P(("dp", "expert"), None),
            P(),
            P(("dp", "expert"), None),
            P(("dp", "expert"), None),
            P(),
            P(("dp", "expert"), None),
            P(("dp", "expert"), None),
            P(("dp", "expert"), None),
            P(),
            P(("dp", "expert"), None),
            P(("dp", "expert"), None),
            P(("dp", "expert"), None),
            P(),
            P(("dp", "expert"), None),
            P(("dp", "expert"), None),
            P(("dp", "expert"), None),
            P("expert", None, None),
            P("expert", "dp", None),
            P("expert", "dp", None),
            P("expert", "dp", None),
            P("expert", None, None),
            P("expert", "dp", None),
            P("expert", "dp", None),
            P("expert", "dp", None),
        ),
        out_specs=(
            P(("dp", "expert"), None),
            P(("dp", "expert"), None),
            P(("dp", "expert"), None),
            P(("dp", "expert"), None),
            P(("dp", "expert"), None),
            P(("dp", "expert"), None),
            P(("dp", "expert"), None),
            P(("dp", "expert"), None),
            P(("dp", "expert"), None),
            P(("dp", "expert"), None),
            P(("dp", "expert"), None),
            P(("dp", "expert"), None),
            P(("dp", "expert"), None),
            P(("dp", "expert"), None),
            P("expert", "dp", None),
            P("expert", "dp", None),
            P("expert", "dp", None),
            P("expert", "dp", None),
            P("expert", "dp", None),
            P("expert", "dp", None),
        ),
        check_vma=False,
    )
```

profile of v0, /device:TPU:0, one launch (start us, length us, event | category | flops | bytes accessed | tf_op | source)
XLA Modules:
  0.0 1631.6 jit_solution(6618232595936007298)
XLA Ops:
  44.7 25.2 %gather_fusion.1 = f32[3072]{0:T(1024)S(1)} fusion(f32[384,16]{0,1:T(8,128)S(1)} %fusion.96, s32[3072]{0:T(1024)S(1)} %reshape.416), kind=kCustom, calls=%fused_computation.5 | custom fusion | bytes 49152 | tf_op jit(solution)/shard_map/jit(take_along_axis)/gather | solution.py:151
  72.1 20.2 %gather_fusion.2 = s32[3072]{0:T(1024)S(1)} fusion(s32[384,16]{1,0:T(8,128)S(1)} %bitcast_subtract_fusion.1, s32[3072]{0:T(1024)S(1)} %reshape.416), kind=kCustom, calls=%fused_computation.6 | custom fusion | bytes 49152 | tf_op jit(solution)/shard_map/jit(take_along_axis)/gather | solution.py:158
  93.5 11.8 scatter_custom_fusion
  105.4 18.3 %gather_fusion.3 = bf16[4096,1024]{1,0:T(8,128)(2,1)} fusion(bf16[384,1024]{1,0:T(8,128)(2,1)S(1)} %multiply_convert_fusion.4, s32[4096]{0:T(1024)S(1)} %fusion.65), kind=kCustom, calls=%fused_computation.clone | custom fusion | bytes 16793600 | tf_op jit(solution)/shard_map/jit(_take)/gather | solution.py:174
  128.1 189.2 %all_to_all.66 = bf16[16,256,1024]{2,1,0:T(8,128)(2,1)} all-to-all(bf16[16,256,1024]{2,1,0:T(8,128)(2,1)S(1)} %bitcast.173), channel_id=1, replica_groups=mesh['dp'=8,'expert'=4] {'expert'}, dimensions={0} | all-to-all | bytes 16777216 | tf_op jit(solution)/shard_map/all_to_all | solution.py:177
  317.3 8.0 copy.198
  325.3 17.0 %fusion.97 = f32[4,1024,1024]{1,2,0:T(8,128)} fusion(bf16[4,1024,1024]{2,1,0:T(8,128)(2,1)} %bitcast.178, bf16[4,1024,1024]{2,1,0:T(8,128)(2,1)} %param.50), kind=kOutput, calls=%fused_computation.204 | convolution fusion | flops 8589934592 | bytes 33554432 | tf_op jit(solution)/shard_map/erd,edf->erf/dot_general | solution.py:178
  342.3 8.5 multiply_convert_fusion.3
  350.9 11.6 convolution_convert_fusion.2
  362.5 22.5 %copy.201 = bf16[4,1024,1024]{2,0,1:T(4,128)(2,1)} copy(bf16[4,1024,1024]{2,1,0:T(8,128)(2,1)} %convolution_convert_fusion.2) | data formatting | bytes 16777216 | tf_op jit(solution)/shard_map/convert_element_type | solution.py:184
  390.8 22.1 %gather_fusion.5 = bf16[4096,1024]{1,0:T(8,128)(2,1)} fusion(bf16[384,1024]{1,0:T(8,128)(2,1)} %param.32, s32[4096]{0:T(1024)S(1)} %fusion.65), kind=kCustom, calls=%fused_computation.2.clone | custom fusion | bytes 16793600 | tf_op jit(solution)/shard_map/jit(_take)/gather | solution.py:194
  412.9 11.8 scatter_custom_fusion.1
  424.8 148.0 %all-to-all-done.1 = bf16[4,1024,1024]{2,0,1:T(4,128)(2,1)} async-done(((bf16[4,1024,1024]{2,0,1:T(4,128)(2,1)}), bf16[4,1024,1024]{2,0,1:T(4,128)(2,1)}, u32[]{:S(2)}, u32[]{:S(2)}) %all-to-all-start.1) | async-done | bytes 8388640 | tf_op jit(solution)/shard_map/all_to_all | solution.py:185
  572.8 9.8 copy.202
  582.6 20.4 %gather_fusion.4 = bf16[3072,1024]{1,0:T(8,128)(2,1)} fusion(bf16[4096,1024]{1,0:T(8,128)(2,1)} %bitcast.168, s32[3072]{0:T(1024)S(1)} %fusion.72), kind=kCustom, calls=%fused_computation.1.clone | custom fusion | bytes 12595200 | tf_op jit(solution)/shard_map/jit(_take)/gather | solution.py:188
  611.0 23.0 %gather_fusion = f32[4096]{0:T(1024)S(1)} fusion(f32[3072]{0:T(1024)S(1)} %div.58, s32[4096]{0:T(1024)S(1)} %fusion.64), kind=kCustom, calls=%fused_computation.4 | custom fusion | bytes 49152 | tf_op jit(solution)/shard_map/jit(_take)/gather | solution.py:170
  649.3 186.8 %all-to-all-done.2 = bf16[16,256,1024]{2,1,0:T(8,128)(2,1)} async-done(((bf16[16,256,1024]{2,1,0:T(8,128)(2,1)}), bf16[16,256,1024]{2,1,0:T(8,128)(2,1)}, u32[]{:S(2)}, u32[]{:S(2)}) %all-to-all-start.2) | async-done | bytes 8388640 | tf_op jit(solution)/shard_map/all_to_all | solution.py:196
  836.1 8.1 copy.204
  844.2 15.5 multiply_convert_fusion.2
  859.7 16.5 %convolution_convert_fusion.1 = bf16[4,1024,1024]{2,1,0:T(8,128)(2,1)} fusion(bf16[4,1024,1024]{2,1,0:T(8,128)(2,1)} %param.50, bf16[4,1024,512]{1,2,0:T(8,128)(2,1)} %get-tuple-element.49, bf16[4,1024,512]{1,2,0:T(8,128)(2,1)} %get-tuple-element.48), kind=kOutput, calls=%fused_computation.27 | convolution fusion | flops 8610906112 | bytes 25165824 | tf_op jit(solution)/shard_map/erf,edf->erd/dot_general | solution.py:219
  876.1 12.1 copy.207
  894.4 11.8 convolution_convert_fusion.3
  906.2 16.3 %convolution_convert_fusion = bf16[4,1024,1024]{2,1,0:T(8,128)(2,1)} fusion(bf16[4,1024,1024]{2,1,0:T(8,128)(2,1)} %bitcast.179, bf16[4,1024,512]{1,2,0:T(8,128)(2,1)} %get-tuple-element.49, bf16[4,1024,512]{1,2,0:T(8,128)(2,1)} %get-tuple-element.48), kind=kOutput, calls=%fused_computation.26 | convolution fusion | flops 8610906112 | bytes 25165824 | tf_op jit(solution)/shard_map/erd,erf->edf/dot_general | solution.py:216
  923.4 11.6 convert_reduce_fusion.1
  935.0 141.3 %all-to-all-done.3 = bf16[4,1024,1024]{2,0,1:T(4,128)(2,1)} async-done(((bf16[4,1024,1024]{2,0,1:T(4,128)(2,1)}), bf16[4,1024,1024]{2,0,1:T(4,128)(2,1)}, u32[]{:S(2)}, u32[]{:S(2)}) %all-to-all-start.3) | async-done | bytes 8388640 | tf_op jit(solution)/shard_map/all_to_all | solution.py:222
  1076.3 9.7 copy.208
  1086.1 20.4 %gather_fusion.6 = bf16[3072,1024]{1,0:T(8,128)(2,1)} fusion(bf16[4096,1024]{1,0:T(8,128)(2,1)} %bitcast.167, s32[3072]{0:T(1024)S(1)} %fusion.72), kind=kCustom, calls=%fused_computation.3.clone | custom fusion | bytes 12595200 | tf_op jit(solution)/shard_map/jit(_take)/gather | solution.py:225
  1121.3 7.9 fusion
  1129.2 11.4 fusion.2
  1182.8 106.7 %reduce-scatter.19.cloned.1.call-done = f32[32,2]{1,0:T(8,128)} async-done(((f32[1024,2]{1,0:T(8,128)}), f32[32,2]{1,0:T(8,128)}) %reduce-scatter.19.cloned.1.call-update) | async-done | bytes 272
  1291.6 144.2 %reduce-scatter.13.cloned.1.call-done = f32[32,1024]{1,0:T(8,128)} async-done(((f32[1024,1024]{1,0:T(8,128)}), f32[32,1024]{1,0:T(8,128)}) %reduce-scatter.13.cloned.1.call-update) | async-done | bytes 131088 | tf_op jit(solution)/shard_map/reduce_scatter | solution.py:289
  1437.5 184.9 %reduce-scatter.11.cloned.1.call-done = f32[32,2048]{1,0:T(8,128)} async-done(((f32[1024,2048]{1,0:T(8,128)}), f32[32,2048]{1,0:T(8,128)}) %reduce-scatter.11.cloned.1.call-update) | async-done | bytes 262160 | tf_op jit(solution)/shard_map/reduce_scatter | solution.py:288
  (259 shorter events, 143.2 us)
Async XLA Ops:
  7.2 32.7 %copy-start = (bf16[1024,1024]{1,0:T(8,128)(2,1)S(1)}, bf16[1024,1024]{1,0:T(8,128)(2,1)}, u32[]{:S(2)}) copy-start(bf16[1024,1024]{1,0:T(8,128)(2,1)} %param.42) | copy-start | bytes 6291460
  8.1 34.3 %copy-start.46 = (f32[1024,1]{0,1:T(1,128)}, f32[1024,1]{0,1:T(1,128)S(1)}, u32[]{:S(2)}) copy-start(f32[1024,1]{0,1:T(1,128)S(1)} %get-tuple-element.66) | copy-start | bytes 12292
  15.1 8.1 copy-start.59
  24.4 7.8 copy-start.17
  24.4 7.8 copy-start.21
  44.6 26.0 %copy-start.45 = (s32[16,3,128]{2,0,1:T(8,128)S(1)}, s32[16,3,128]{2,0,1:T(8,128)}, u32[]{:S(2)}) copy-start(s32[16,3,128]{2,0,1:T(8,128)} %copy_bitcast_fusion) | copy-start | bytes 73732
  44.6 27.4 %copy-start.25 = (s32[384,16]{1,0:T(8,128)S(1)}, s32[384,16]{1,0:T(8,128)}, u32[]{:S(2)}) copy-start(s32[384,16]{1,0:T(8,128)} %copy.194) | copy-start | bytes 73732
  385.0 187.8 %all-to-all-start.1 = ((bf16[4,1024,1024]{2,0,1:T(4,128)(2,1)}), bf16[4,1024,1024]{2,0,1:T(4,128)(2,1)}, u32[]{:S(2)}, u32[]{:S(2)}) async-start(bf16[4,1024,1024]{2,0,1:T(4,128)(2,1)} %copy.201), calls=%async_computation.1 | async-start | bytes 16777216 | tf_op jit(solution)/shard_map/all_to_all | solution.py:185
  390.7 34.0 %copy-start.39 = (f32[384,8]{0,1:T(8,128)S(1)}, f32[384,8]{0,1:T(8,128)}, u32[]{:S(2)}) copy-start(f32[384,8]{0,1:T(8,128)} %copy-done.38) | copy-start | bytes 36868
  390.8 34.0 %copy-start.53 = (f32[384]{0:T(512)S(1)}, f32[384]{0:T(512)}, u32[]{:S(2)}) copy-start(f32[384]{0:T(512)} %get-tuple-element.46) | copy-start | bytes 4612
  641.9 194.2 %all-to-all-start.2 = ((bf16[16,256,1024]{2,1,0:T(8,128)(2,1)}), bf16[16,256,1024]{2,1,0:T(8,128)(2,1)}, u32[]{:S(2)}, u32[]{:S(2)}) async-start(bf16[16,256,1024]{2,1,0:T(8,128)(2,1)} %bitcast.174), calls=%async_computation.2 | async-start | bytes 16777216 | tf_op jit(solution)/shard_map/all_to_all | solution.py:196
  647.5 520.8 %reduce-scatter.21.cloned.1.call-start = ((), (), s32[]{:S(2)}) async-start(), calls=%async_computation.15 | async-start | bytes 540672
  888.3 188.1 %all-to-all-start.3 = ((bf16[4,1024,1024]{2,0,1:T(4,128)(2,1)}), bf16[4,1024,1024]{2,0,1:T(4,128)(2,1)}, u32[]{:S(2)}, u32[]{:S(2)}) async-start(bf16[4,1024,1024]{2,0,1:T(4,128)(2,1)} %copy.207), calls=%async_computation.3 | async-start | bytes 16777216 | tf_op jit(solution)/shard_map/all_to_all | solution.py:222
  893.9 275.8 %reduce-scatter.17.cloned.1.call-start = ((), (), s32[]{:S(2)}) async-start(), calls=%async_computation.13 | async-start | bytes 4718592 | tf_op jit(solution)/shard_map/reduce_scatter | solution.py:297
  906.2 269.4 %reduce-scatter.15.cloned.1.call-start = ((), (), s32[]{:S(2)}) async-start(), calls=%async_computation.12 | async-start | bytes 9437184 | tf_op jit(solution)/shard_map/reduce_scatter | solution.py:294
  922.6 366.9 %reduce-scatter.19.cloned.1.call-start = ((), (), s32[]{:S(2)}) async-start(), calls=%async_computation.14 | async-start | bytes 540672
  1106.5 7.3 copy-start.5
  1106.5 7.3 copy-start.41
  1106.5 7.3 copy-start.47
  1106.5 7.3 copy-start.52
  1121.3 7.9 copy-start.14
  1129.2 11.4 copy-start.11
  1155.7 280.0 %reduce-scatter.13.cloned.1.call-start = ((), (), s32[]{:S(2)}) async-start(), calls=%async_computation.11 | async-start | bytes 4325376 | tf_op jit(solution)/shard_map/reduce_scatter | solution.py:289
  1160.7 461.6 %reduce-scatter.11.cloned.1.call-start = ((), (), s32[]{:S(2)}) async-start(), calls=%async_computation.10 | async-start | bytes 8650752 | tf_op jit(solution)/shard_map/reduce_scatter | solution.py:288
  1175.5 114.7 %copy-start.57 = (f32[32,2]{0,1:T(2,128)S(1)}, f32[32,2]{0,1:T(2,128)}, u32[]{:S(2)}) copy-start(f32[32,2]{0,1:T(2,128)} %param.37) | copy-start | bytes 772
  1175.5 114.7 %copy-start.58 = (f32[32,2]{0,1:T(2,128)S(1)}, f32[32,2]{0,1:T(2,128)}, u32[]{:S(2)}) copy-start(f32[32,2]{0,1:T(2,128)} %param.36) | copy-start | bytes 772
  1175.5 260.2 %copy-start.42 = (f32[32,1024]{1,0:T(8,128)S(1)}, f32[32,1024]{1,0:T(8,128)}, u32[]{:S(2)}) copy-start(f32[32,1024]{1,0:T(8,128)} %param.45) | copy-start | bytes 393220
  1175.5 260.2 %copy-start.43 = (f32[32,1024]{1,0:T(8,128)S(1)}, f32[32,1024]{1,0:T(8,128)}, u32[]{:S(2)}) copy-start(f32[32,1024]{1,0:T(8,128)} %param.43) | copy-start | bytes 393220
  1175.5 260.2 %copy-start.44 = (f32[32,1024]{1,0:T(8,128)S(1)}, f32[32,1024]{1,0:T(8,128)}, u32[]{:S(2)}) copy-start(f32[32,1024]{1,0:T(8,128)} %param.44) | copy-start | bytes 393220
  1175.6 446.8 %copy-start.31 = (f32[32,2048]{1,0:T(8,128)S(1)}, f32[32,2048]{1,0:T(8,128)}, u32[]{:S(2)}) copy-start(f32[32,2048]{1,0:T(8,128)} %param.41) | copy-start | bytes 786436
  1175.6 446.8 %copy-start.32 = (f32[32,2048]{1,0:T(8,128)S(1)}, f32[32,2048]{1,0:T(8,128)}, u32[]{:S(2)}) copy-start(f32[32,2048]{1,0:T(8,128)} %param.39) | copy-start | bytes 786436
  1175.6 446.8 %copy-start.33 = (f32[32,2048]{1,0:T(8,128)S(1)}, f32[32,2048]{1,0:T(8,128)}, u32[]{:S(2)}) copy-start(f32[32,2048]{1,0:T(8,128)} %param.40) | copy-start | bytes 786436
  (43 other events, 120.8 us)
Sparse Core Ops, SparseCore 0:
  651.1 243.6 reduce-scatter.20
  906.3 52.8 reduce-scatter.16
  962.6 71.2 reduce-scatter.14
  1155.9 133.5 reduce-scatter.18
  1291.6 144.1 reduce-scatter.12
  1437.9 184.4 reduce-scatter.10
where the time goes:
time: 1640 us; the launch traced here: 1630 us
  waiting for transfers between devices  912 us (56%)
  local copies, waits for them, and re-layouts  267 us (16%)
  blocking collectives  189 us (12%)
  matrix products  161 us (10%)
  other arithmetic  68.7 us (4%)
  starting transfers between devices  17.9 us (1%)
    all_to_all x1, blocking collectives, body(): lax.all_to_all(outgoing, 'expert', split_axis=0, concat_axis=1, tiled=True)  189 us
    all_to_all x1, waiting for transfers between devices, body(): lax.all_to_all(outgoing_grads.reshape(experts, capacity, model_width), 'e...  187 us
    reduce_scatter x1, waiting for transfers between devices, body(): lax.psum_scatter(grad_heads_in, ('dp', 'expert'), scatter_dimension=0, ti...  185 us
    all_to_all x1, waiting for transfers between devices, body(): lax.all_to_all(result, 'expert', split_axis=1, concat_axis=0, tiled=True)  148 us
    reduce_scatter x1, waiting for transfers between devices, body(): lax.psum_scatter(grad_heads_out, ('dp', 'expert'), scatter_dimension=0, t...  144 us
    all_to_all x1, waiting for transfers between devices, body(): lax.all_to_all(grad_inputs, 'expert', split_axis=1, concat_axis=0, tiled=...  141 us
    unnamed x8, waiting for transfers between devices  107 us
  transfers between devices with their start and end apart: 9, of which 6 were waited for; matrix products, arithmetic and copies ran while one was open for 14% of the time, Pallas kernels for 0%

commit v1 on v0

--- a/solution.py
+++ b/solution.py
@@ -2,6 +2,7 @@
 import jax.numpy as jnp
 from jax import lax
 from jax.sharding import PartitionSpec as P
+from jax.lax import axis_index, axis_size, ppermute
 
 HEADS = 16
 KV_HEADS = 8
@@ -13,6 +14,24 @@
 DECAY = 0.8
 RATE = 0.001
 HIGHEST = lax.Precision.HIGHEST
+
+
+def supply_loads(block_in, which_dim, z_in):
+    mat_out = block_in.shape
+    part_now = block_in.reshape(
+        *mat_out[:which_dim], z_in, mat_out[which_dim] // z_in, *mat_out[which_dim + 1 :]
+    )
+    back = jnp.moveaxis(part_now, which_dim, 0)
+    return back
+
+
+def close_shapes(z, along_dim):
+    z = jnp.moveaxis(z, 0, along_dim)
+    h_now = z.shape
+    found_now = z.reshape(
+        *h_now[:along_dim], h_now[along_dim] * h_now[along_dim + 1], *h_now[along_dim + 2 :]
+    )
+    return found_now
 
 
 def layout(labels_row, prompt_len):
@@ -219,9 +238,23 @@
     grad_inputs = jnp.einsum(
         "erf,edf->erd", grad_gate_up, expert_in, preferred_element_type=jnp.float32
     ).astype(jnp.bfloat16)
-    returned_grads = lax.all_to_all(
-        grad_inputs, "expert", split_axis=1, concat_axis=0, tiled=True
-    ).reshape(experts * capacity, model_width)
+
+    def task_define(across, work_x, m, a0):
+        opened, v_now = (axis_size(across), axis_index(across))
+        new = supply_loads(m, work_x, opened)
+        vals = [new[v_now]]
+        for no in [*range(1, opened)]:
+            lower = new[v_now ^ no]
+            vals.append(
+                ppermute(lower, axis_name=across, perm=[(ix, ix ^ no) for ix in range(opened)])
+            )
+        new = jnp.stack(vals)[v_now ^ jnp.arange(opened)]
+        outer = close_shapes(new, a0)
+        return outer
+
+    returned_grads = task_define("expert", 1, grad_inputs, 0).reshape(
+        experts * capacity, model_width
+    )
     gathered_grads = jnp.take(returned_grads, flat_rows.reshape(-1), axis=0).reshape(
         token_count, fanout, model_width
     )

time: 1640 us -> 1770 us (1.079)
  waiting for transfers between devices: 912 us -> 1040 us
    all_to_all x1 -> x0, waiting for transfers between devices: 141 us -> none  [body(): lax.all_to_all(grad_inputs, 'expert', split_axis=1, concat_axis=0, tiled=...]
    ppermute x0 -> x3, waiting for transfers between devices: none -> 123 us  [task_define(): ppermute(lower, axis_name=across, perm=[(ix, ix ^ no) for ix in range(ope...]
    reduce_scatter x1, waiting for transfers between devices: 0.02 us -> 72 us  [body(): lax.psum_scatter(grad_expert_in.astype(jnp.bfloat16), 'dp', scatter_dimen...]
    reduce_scatter x1, waiting for transfers between devices: 0.01 us -> 48.9 us  [body(): lax.psum_scatter(grad_expert_out.astype(jnp.bfloat16), 'dp', scatter_dime...]
    unnamed x8, waiting for transfers between devices: 107 us -> 134 us
  transfers between devices with their start and end apart: 9 -> 11, of which waited for: 6 -> 9; matrix products, arithmetic and copies ran while one was open for 14% -> 11% of each run, Pallas kernels for 0% -> 0%
where the time goes in v1:
time: 1770 us; the launch traced here: 1760 us
  waiting for transfers between devices  1040 us (59%)
  local copies, waits for them, and re-layouts  251 us (14%)
  blocking collectives  189 us (11%)
  matrix products  164 us (9%)
  other arithmetic  81.9 us (5%)
    all_to_all x1, blocking collectives, body(): lax.all_to_all(outgoing, 'expert', split_axis=0, concat_axis=1, tiled=True)  189 us
    all_to_all x1, waiting for transfers between devices, body(): lax.all_to_all(outgoing_grads.reshape(experts, capacity, model_width), 'e...  182 us
    reduce_scatter x1, waiting for transfers between devices, body(): lax.psum_scatter(grad_heads_in, ('dp', 'expert'), scatter_dimension=0, ti...  181 us
    all_to_all x1, waiting for transfers between devices, body(): lax.all_to_all(result, 'expert', split_axis=1, concat_axis=0, tiled=True)  152 us
    reduce_scatter x1, waiting for transfers between devices, body(): lax.psum_scatter(grad_heads_out, ('dp', 'expert'), scatter_dimension=0, t...  146 us
    unnamed x8, waiting for transfers between devices  134 us
    ppermute x3, waiting for transfers between devices, task_define(): ppermute(lower, axis_name=across, perm=[(ix, ix ^ no) for ix in range(ope...  123 us
    reduce_scatter x1, waiting for transfers between devices, body(): lax.psum_scatter(grad_expert_in.astype(jnp.bfloat16), 'dp', scatter_dimen...  72 us
  transfers between devices with their start and end apart: 11, of which 9 were waited for; matrix products, arithmetic and copies ran while one was open for 11% of the time, Pallas kernels for 0%

profile of v1, /device:TPU:0, one launch (start us, length us, event | category | flops | bytes accessed | tf_op | source)
XLA Modules:
  0.0 1757.7 jit_solution(8017710401255701486)
XLA Ops:
  44.6 25.3 %gather_fusion.1 = f32[3072]{0:T(1024)S(1)} fusion(f32[384,16]{0,1:T(8,128)S(1)} %fusion.100, s32[3072]{0:T(1024)S(1)} %reshape.438), kind=kCustom, calls=%fused_computation.5 | custom fusion | bytes 49152 | tf_op jit(solution)/shard_map/jit(take_along_axis)/gather | solution.py:170
  72.1 20.2 %gather_fusion.2 = s32[3072]{0:T(1024)S(1)} fusion(s32[384,16]{1,0:T(8,128)S(1)} %bitcast_subtract_fusion.1, s32[3072]{0:T(1024)S(1)} %reshape.438), kind=kCustom, calls=%fused_computation.6 | custom fusion | bytes 49152 | tf_op jit(solution)/shard_map/jit(take_along_axis)/gather | solution.py:177
  93.6 11.8 scatter_custom_fusion
  105.5 18.3 %gather_fusion.5 = bf16[4096,1024]{1,0:T(8,128)(2,1)} fusion(bf16[384,1024]{1,0:T(8,128)(2,1)S(1)} %multiply_convert_fusion.4, s32[4096]{0:T(1024)S(1)} %fusion.65), kind=kCustom, calls=%fused_computation.clone | custom fusion | bytes 16793600 | tf_op jit(solution)/shard_map/jit(_take)/gather | solution.py:193
  128.2 189.2 %all_to_all.51 = bf16[16,256,1024]{2,1,0:T(8,128)(2,1)} all-to-all(bf16[16,256,1024]{2,1,0:T(8,128)(2,1)S(1)} %bitcast.184), channel_id=1, replica_groups=mesh['dp'=8,'expert'=4] {'expert'}, dimensions={0} | all-to-all | bytes 16777216 | tf_op jit(solution)/shard_map/all_to_all | solution.py:196
  325.4 17.0 fusion.101
  342.4 8.5 multiply_convert_fusion.3
  351.0 11.6 convolution_convert_fusion.2
  362.6 12.3 copy.195
  380.8 18.2 %gather_fusion.7 = bf16[4096,1024]{1,0:T(8,128)(2,1)} fusion(bf16[384,1024]{1,0:T(8,128)(2,1)S(1)} %copy-done.3, s32[4096]{0:T(1024)S(1)} %fusion.65), kind=kCustom, calls=%fused_computation.2.clone | custom fusion | bytes 16793600 | tf_op jit(solution)/shard_map/jit(_take)/gather | solution.py:213
  399.0 11.8 scatter_custom_fusion.1
  410.9 152.0 %all-to-all-done.1 = bf16[4,1024,1024]{2,0,1:T(4,128)(2,1)} async-done(((bf16[4,1024,1024]{2,0,1:T(4,128)(2,1)}), bf16[4,1024,1024]{2,0,1:T(4,128)(2,1)}, u32[]{:S(2)}, u32[]{:S(2)}) %all-to-all-start.1) | async-done | bytes 8388640 | tf_op jit(solution)/shard_map/all_to_all | solution.py:204
  562.8 9.8 copy.196
  572.6 20.4 %gather_fusion.6 = bf16[3072,1024]{1,0:T(8,128)(2,1)} fusion(bf16[4096,1024]{1,0:T(8,128)(2,1)} %bitcast.179, s32[3072]{0:T(1024)S(1)} %fusion.72), kind=kCustom, calls=%fused_computation.1.clone | custom fusion | bytes 12595200 | tf_op jit(solution)/shard_map/jit(_take)/gather | solution.py:207
  599.8 23.0 %gather_fusion = f32[4096]{0:T(1024)S(1)} fusion(f32[3072]{0:T(1024)S(1)} %div.58, s32[4096]{0:T(1024)S(1)} %fusion.64), kind=kCustom, calls=%fused_computation.4 | custom fusion | bytes 49152 | tf_op jit(solution)/shard_map/jit(_take)/gather | solution.py:189
  636.5 182.3 %all-to-all-done.2 = bf16[16,256,1024]{2,1,0:T(8,128)(2,1)} async-done(((bf16[16,256,1024]{2,1,0:T(8,128)(2,1)}), bf16[16,256,1024]{2,1,0:T(8,128)(2,1)}, u32[]{:S(2)}, u32[]{:S(2)}) %all-to-all-start.2) | async-done | bytes 8388640 | tf_op jit(solution)/shard_map/all_to_all | solution.py:215
  818.8 8.0 copy.198
  826.8 15.2 multiply_convert_fusion.2
  842.1 16.4 convolution_convert_fusion.1
  872.1 12.2 convert_reduce_fusion.1
  884.3 75.0 %collective-permute-done = bf16[4,256,1024]{2,1,0:T(8,128)(2,1)} collective-permute-done((bf16[4,256,1024]{2,1,0:T(8,128)(2,1)}, bf16[4,256,1024]{2,1,0:T(8,128)(2,1)}, u32[]{:S(2)}, u32[]{:S(2)}) %collective-permute-start) | collective-permute-done | bytes 2097184 | tf_op jit(solution)/shard_map/ppermute | solution.py:249
  959.2 48.2 %collective-permute-done.1 = bf16[4,256,1024]{2,1,0:T(8,128)(2,1)} collective-permute-done((bf16[4,256,1024]{2,1,0:T(8,128)(2,1)}, bf16[4,256,1024]{2,1,0:T(8,128)(2,1)}, u32[]{:S(2)}, u32[]{:S(2)}) %collective-permute-start.1) | collective-permute-done | bytes 2097184 | tf_op jit(solution)/shard_map/ppermute | solution.py:249
  1033.1 20.4 %gather_fusion.8 = bf16[3072,1024]{1,0:T(8,128)(2,1)} fusion(bf16[4096,1024]{1,0:T(8,128)(2,1)} %bitcast.178, s32[3072]{0:T(1024)S(1)} %fusion.72), kind=kCustom, calls=%fused_computation.3.clone | custom fusion | bytes 12595200 | tf_op jit(solution)/shard_map/jit(_take)/gather | solution.py:258
  1069.0 10.5 fusion
  1082.7 11.2 fusion.2
  1105.9 11.7 convolution_convert_fusion.3
  1122.7 16.7 convolution_convert_fusion
  1151.4 134.3 %reduce-scatter.19.cloned.1.call-done = f32[32,2]{1,0:T(8,128)} async-done(((f32[1024,2]{1,0:T(8,128)}), f32[32,2]{1,0:T(8,128)}) %reduce-scatter.19.cloned.1.call-update) | async-done | bytes 272
  1287.8 48.9 %reduce-scatter.17.cloned.1.call-done = bf16[4,128,512]{2,1,0:T(8,128)(2,1)} async-done(((bf16[4,1024,512]{2,1,0:T(8,128)(2,1)}), bf16[4,128,512]{2,1,0:T(8,128)(2,1)}) %reduce-scatter.17.cloned.1.call-update) | async-done | bytes 524304 | tf_op jit(solution)/shard_map/reduce_scatter | solution.py:330
  1340.8 146.0 %reduce-scatter.13.cloned.1.call-done = f32[32,1024]{1,0:T(8,128)} async-done(((f32[1024,1024]{1,0:T(8,128)}), f32[32,1024]{1,0:T(8,128)}) %reduce-scatter.13.cloned.1.call-update) | async-done | bytes 131088 | tf_op jit(solution)/shard_map/reduce_scatter | solution.py:322
  1488.5 72.0 %reduce-scatter.15.cloned.1.call-done = bf16[4,128,1024]{2,1,0:T(8,128)(2,1)} async-done(((bf16[4,1024,1024]{2,1,0:T(8,128)(2,1)}), bf16[4,128,1024]{2,1,0:T(8,128)(2,1)}) %reduce-scatter.15.cloned.1.call-update) | async-done | bytes 1048592 | tf_op jit(solution)/shard_map/reduce_scatter | solution.py:327
  1567.5 181.0 %reduce-scatter.11.cloned.1.call-done = f32[32,2048]{1,0:T(8,128)} async-done(((f32[1024,2048]{1,0:T(8,128)}), f32[32,2048]{1,0:T(8,128)}) %reduce-scatter.11.cloned.1.call-update) | async-done | bytes 262160 | tf_op jit(solution)/shard_map/reduce_scatter | solution.py:321
  (271 shorter events, 182.6 us)
Async XLA Ops:
  7.2 32.7 %copy-start = (bf16[1024,1024]{1,0:T(8,128)(2,1)S(1)}, bf16[1024,1024]{1,0:T(8,128)(2,1)}, u32[]{:S(2)}) copy-start(bf16[1024,1024]{1,0:T(8,128)(2,1)} %param.42) | copy-start | bytes 6291460
  8.1 34.3 %copy-start.47 = (f32[1024,1]{0,1:T(1,128)}, f32[1024,1]{0,1:T(1,128)S(1)}, u32[]{:S(2)}) copy-start(f32[1024,1]{0,1:T(1,128)S(1)} %get-tuple-element.72) | copy-start | bytes 12292
  44.3 61.1 %copy-start.1 = (bf16[384,1024]{1,0:T(8,128)(2,1)}, bf16[384,1024]{1,0:T(8,128)(2,1)S(1)}, u32[]{:S(2)}) copy-start(bf16[384,1024]{1,0:T(8,128)(2,1)S(1)} %multiply_convert_fusion.4) | copy-start | bytes 2359300
  44.6 26.1 %copy-start.46 = (s32[16,3,128]{2,0,1:T(8,128)S(1)}, s32[16,3,128]{2,0,1:T(8,128)}, u32[]{:S(2)}) copy-start(s32[16,3,128]{2,0,1:T(8,128)} %copy_bitcast_fusion) | copy-start | bytes 73732
  44.6 27.5 %copy-start.25 = (s32[384,16]{1,0:T(8,128)S(1)}, s32[384,16]{1,0:T(8,128)}, u32[]{:S(2)}) copy-start(s32[384,16]{1,0:T(8,128)} %copy.188) | copy-start | bytes 73732
  374.9 187.9 %all-to-all-start.1 = ((bf16[4,1024,1024]{2,0,1:T(4,128)(2,1)}), bf16[4,1024,1024]{2,0,1:T(4,128)(2,1)}, u32[]{:S(2)}, u32[]{:S(2)}) async-start(bf16[4,1024,1024]{2,0,1:T(4,128)(2,1)} %copy.195), calls=%async_computation.1 | async-start | bytes 16777216 | tf_op jit(solution)/shard_map/all_to_all | solution.py:204
  380.7 30.0 %copy-start.40 = (f32[384,8]{0,1:T(8,128)S(1)}, f32[384,8]{0,1:T(8,128)}, u32[]{:S(2)}) copy-start(f32[384,8]{0,1:T(8,128)} %copy-done.39) | copy-start | bytes 36868
  380.7 30.0 %copy-start.54 = (f32[384]{0:T(512)S(1)}, f32[384]{0:T(512)}, u32[]{:S(2)}) copy-start(f32[384]{0:T(512)} %get-tuple-element.46) | copy-start | bytes 4612
  630.7 188.1 %all-to-all-start.2 = ((bf16[16,256,1024]{2,1,0:T(8,128)(2,1)}), bf16[16,256,1024]{2,1,0:T(8,128)(2,1)}, u32[]{:S(2)}, u32[]{:S(2)}) async-start(bf16[16,256,1024]{2,1,0:T(8,128)(2,1)} %bitcast.185), calls=%async_computation.2 | async-start | bytes 16777216 | tf_op jit(solution)/shard_map/all_to_all | solution.py:215
  636.2 510.3 %reduce-scatter.21.cloned.1.call-start = ((), (), s32[]{:S(2)}) async-start(), calls=%async_computation.14 | async-start | bytes 540672
  858.5 11.5 copy-start.51
  858.5 11.7 copy-start.31
  858.5 11.7 copy-start.2
  865.6 93.6 %collective-permute-start = (bf16[4,256,1024]{2,1,0:T(8,128)(2,1)}, bf16[4,256,1024]{2,1,0:T(8,128)(2,1)}, u32[]{:S(2)}, u32[]{:S(2)}) collective-permute-start(bf16[4,256,1024]{2,1,0:T(8,128)(2,1)} %get-tuple-element.55), channel_id=1, source_target_pairs={{0,1},{1,0},{2,3},{3,2},{4,5},{5,4},{6,7},{7,6},{8,9},{9,8},{10,11... | collective-permute-start | bytes 6291464 | tf_op jit(solution)/shard_map/ppermute | solution.py:249
  865.6 141.8 %collective-permute-start.1 = (bf16[4,256,1024]{2,1,0:T(8,128)(2,1)}, bf16[4,256,1024]{2,1,0:T(8,128)(2,1)}, u32[]{:S(2)}, u32[]{:S(2)}) collective-permute-start(bf16[4,256,1024]{2,1,0:T(8,128)(2,1)} %get-tuple-element.54), channel_id=1, source_target_pairs={{0,2},{1,3},{2,0},{3,1},{4,6},{5,7},{6,4},{7,5},{8,10},{9,11},{10,... | collective-permute-start | bytes 6291464 | tf_op jit(solution)/shard_map/ppermute | solution.py:249
  867.7 139.8 %collective-permute-start.2 = (bf16[4,256,1024]{2,1,0:T(8,128)(2,1)}, bf16[4,256,1024]{2,1,0:T(8,128)(2,1)}, u32[]{:S(2)}, u32[]{:S(2)}) collective-permute-start(bf16[4,256,1024]{2,1,0:T(8,128)(2,1)} %get-tuple-element.53), channel_id=1, source_target_pairs={{0,3},{1,2},{2,1},{3,0},{4,7},{5,6},{6,5},{7,4},{8,11},{9,10},{10,... | collective-permute-start | bytes 6291464 | tf_op jit(solution)/shard_map/ppermute | solution.py:249
  872.0 413.7 %reduce-scatter.19.cloned.1.call-start = ((), (), s32[]{:S(2)}) async-start(), calls=%async_computation.13 | async-start | bytes 540672
  872.1 135.3 %copy-start.8 = (bf16[1,4,256,1024]{3,2,1,0:T(8,128)(2,1)S(1)}, bf16[1,4,256,1024]{3,2,1,0:T(8,128)(2,1)}, u32[]{:S(2)}) copy-start(bf16[1,4,256,1024]{3,2,1,0:T(8,128)(2,1)} %get-tuple-element.52) | copy-start | bytes 6291460
  1064.9 14.7 slice-start
  1082.7 11.2 copy-start.14
  1105.8 230.9 %reduce-scatter.17.cloned.1.call-start = ((), (), s32[]{:S(2)}) async-start(), calls=%async_computation.12 | async-start | bytes 4718592 | tf_op jit(solution)/shard_map/reduce_scatter | solution.py:330
  1117.6 369.2 %reduce-scatter.13.cloned.1.call-start = ((), (), s32[]{:S(2)}) async-start(), calls=%async_computation.10 | async-start | bytes 4325376 | tf_op jit(solution)/shard_map/reduce_scatter | solution.py:322
  1122.6 437.9 %reduce-scatter.15.cloned.1.call-start = ((), (), s32[]{:S(2)}) async-start(), calls=%async_computation.11 | async-start | bytes 9437184 | tf_op jit(solution)/shard_map/reduce_scatter | solution.py:327
  1139.4 609.1 %reduce-scatter.11.cloned.1.call-start = ((), (), s32[]{:S(2)}) async-start(), calls=%async_computation.9 | async-start | bytes 8650752 | tf_op jit(solution)/shard_map/reduce_scatter | solution.py:321
  1146.5 140.0 %copy-start.58 = (f32[32,2]{0,1:T(2,128)S(1)}, f32[32,2]{0,1:T(2,128)}, u32[]{:S(2)}) copy-start(f32[32,2]{0,1:T(2,128)} %param.37) | copy-start | bytes 772
  1146.5 140.0 %copy-start.59 = (f32[32,2]{0,1:T(2,128)S(1)}, f32[32,2]{0,1:T(2,128)}, u32[]{:S(2)}) copy-start(f32[32,2]{0,1:T(2,128)} %param.36) | copy-start | bytes 772
  1151.4 335.4 %copy-start.43 = (f32[32,1024]{1,0:T(8,128)S(1)}, f32[32,1024]{1,0:T(8,128)}, u32[]{:S(2)}) copy-start(f32[32,1024]{1,0:T(8,128)} %param.45) | copy-start | bytes 393220
  1151.4 335.4 %copy-start.44 = (f32[32,1024]{1,0:T(8,128)S(1)}, f32[32,1024]{1,0:T(8,128)}, u32[]{:S(2)}) copy-start(f32[32,1024]{1,0:T(8,128)} %param.43) | copy-start | bytes 393220
  1151.4 335.4 %copy-start.45 = (f32[32,1024]{1,0:T(8,128)S(1)}, f32[32,1024]{1,0:T(8,128)}, u32[]{:S(2)}) copy-start(f32[32,1024]{1,0:T(8,128)} %param.44) | copy-start | bytes 393220
  1488.5 260.0 %copy-start.32 = (f32[32,2048]{1,0:T(8,128)S(1)}, f32[32,2048]{1,0:T(8,128)}, u32[]{:S(2)}) copy-start(f32[32,2048]{1,0:T(8,128)} %param.41) | copy-start | bytes 786436
  1488.5 260.0 %copy-start.33 = (f32[32,2048]{1,0:T(8,128)S(1)}, f32[32,2048]{1,0:T(8,128)}, u32[]{:S(2)}) copy-start(f32[32,2048]{1,0:T(8,128)} %param.39) | copy-start | bytes 786436
  1488.5 260.0 %copy-start.34 = (f32[32,2048]{1,0:T(8,128)S(1)}, f32[32,2048]{1,0:T(8,128)}, u32[]{:S(2)}) copy-start(f32[32,2048]{1,0:T(8,128)} %param.40) | copy-start | bytes 786436
  (46 other events, 180.0 us)
Sparse Core Ops, SparseCore 0:
  872.2 237.9 reduce-scatter.20
  1113.1 172.5 reduce-scatter.18
  1289.1 47.6 reduce-scatter.16
  1339.0 147.7 reduce-scatter.12
  1490.5 69.9 reduce-scatter.14
  1562.7 185.7 reduce-scatter.10
